TPU v7x, 32 devices: a whole 2x2x4 slice. The times are simulated.
32 devices in a mesh: groups: 2 (over x), hid: 8 (over z, y), wid: 2 (over core).
Axes of the slice: x: 2, y: 2, z: 4, core: 2. Of those that a mesh axis runs over, the one named last changes fastest.
Arguments:
- tokens: bfloat16 [256, 18432], P(('groups', 'hid'), 'wid'), parts along dimension 0, may hold values from -180 to 180
- norm_gain: float32 [18432], P('wid'), may hold values from 0.1 to 1.9
- query_weight: bfloat16 [18432, 8192], P('wid', 'hid'), may hold values from -0.046875 to 0.046875
- query_scale: float32 [8192], P('hid'), may hold values from 0.5 to 2
- kv_weight: bfloat16 [18432, 512], P('wid'), may hold values from -0.046875 to 0.046875
- kv_scale: float32 [512], replicated, may hold values from 0.5 to 2
- keys_cache: bfloat16 [256, 512, 256], P(('groups', 'hid', 'wid')), parts along dimension 0, may hold values from -384 to 384
- values_cache: bfloat16 [256, 512, 256], P(('groups', 'hid', 'wid')), parts along dimension 0, may hold values from -6 to 6
- lengths: int32 [256], P(('groups', 'hid', 'wid')), parts along dimension 0, may hold values from 1 to 512, as said below
Outputs:
- attended: bfloat16 [256, 8192], P(('groups', 'hid', 'wid')), parts along dimension 0
- new_entries: bfloat16 [256, 512], P(('groups', 'hid', 'wid')), parts along dimension 0
There are 2 independent parts, one for each index of `groups`. A program takes and returns all parts, laid end to end along the dimension named above; an argument that names none is the same for every part. Nothing has to cross between parts.
Inputs may be any that keep to these rules, and one draw needn't show every extreme that they name: `lengths`: in one aligned block of 8 requests every length is 512.
All inputs are finite; a program needn't handle non-finite values.
Results may differ from a plain program's by a relative error of at most 0.009.
The roundings to bfloat16 on the way count: a program that leaves them out, or rounds other values in their place, can miss the bound.
Values may be sent and summed in bfloat16 or wider, within the bound.
A program may use at most 128 MiB of HBM per device.

v0:
```python
import functools

import jax
import jax.numpy as jnp
from jax import lax
from jax.experimental import pallas as pl
from jax.experimental.pallas import tpu as pltpu
from jax.sharding import PartitionSpec as P

EPSILON = 1e-05
CHUNKS = 4
ROWS_Y = 2
UP, DOWN, SIDE = 0, 1, 2
MESH = pl.DeviceIdType.MESH


def kernel(
    hid_count, wid_count,
    tok_hbm, gain_hbm, qw_hbm, qs_hbm, kw_hbm, ks_hbm, keys_hbm, vals_hbm, len_ref,
    att_ref, new_ref,
    gat, gain, qw, qs, kw, ks, keys, vals,
    stat_mine, stat_other, stats, normed, acc, acc_rx, kv_acc, kv_rx, kv_new,
    q_tx, q_rx, q_f32, o_f32, att,
    tok_sem, qw_sem, kw_sem, misc_sem,
    send_sem, recv_sem, pair_sem, acc_send, acc_recv, q_send, q_recv, out_sem,
):
    own_rows, half_width = tok_hbm.shape
    full_width = half_width * wid_count
    width = half_width // CHUNKS
    tiles, _, _, req, head_dim = acc.shape
    z_count = hid_count // ROWS_Y
    me = lax.axis_index("hid")
    core = lax.axis_index("wid")
    other = 1 - core
    z = me // ROWS_Y
    y = lax.rem(me, ROWS_Y)
    side = z * ROWS_Y + (1 - y)

    def hid_at(zz, yy):
        return zz * ROWS_Y + yy

    def cols(c):
        return pl.ds(pl.multiple_of(c * width, 128), width)

    def tok_copy(c):
        return pltpu.make_async_copy(tok_hbm.at[:, cols(c)], gat.at[me, c], tok_sem.at[c])

    def kw_copy(c):
        return pltpu.make_async_copy(kw_hbm.at[cols(c)], kw.at[c], kw_sem.at[c])

    def qw_copy(c):
        return pltpu.make_async_copy(qw_hbm.at[cols(c)], qw.at[c], qw_sem.at[c])

    small = [
        pltpu.make_async_copy(gain_hbm, gain, misc_sem.at[0]),
        pltpu.make_async_copy(qs_hbm, qs, misc_sem.at[1]),
        pltpu.make_async_copy(ks_hbm, ks, misc_sem.at[2]),
        pltpu.make_async_copy(keys_hbm, keys, misc_sem.at[3]),
        pltpu.make_async_copy(vals_hbm, vals, misc_sem.at[4]),
    ]
    for c in range(CHUNKS):
        tok_copy(c).start()
    for copy in small[:3]:
        copy.start()

    barrier = pltpu.get_barrier_semaphore()

    @pl.when(z + 1 < z_count)
    def _():
        pl.semaphore_signal(barrier, inc=1, device_id={"hid": hid_at(z + 1, y)}, device_id_type=MESH)

    @pl.when(z > 0)
    def _():
        pl.semaphore_signal(barrier, inc=1, device_id={"hid": hid_at(z - 1, y)}, device_id_type=MESH)

    pl.semaphore_signal(barrier, inc=1, device_id={"hid": side}, device_id_type=MESH)
    pl.semaphore_signal(barrier, inc=1, device_id={"wid": other}, device_id_type=MESH)
    for c in range(CHUNKS):
        kw_copy(c).start()
    for c in range(CHUNKS):
        qw_copy(c).start()
    for copy in small[3:]:
        copy.start()

    def block_at(h, c):
        return stats.at[h] if isinstance(c, int) and c == CHUNKS else gat.at[h, c]

    def send(h, c, link, src=None):
        if link == UP:
            target = hid_at(z + 1, y)
        elif link == DOWN:
            target = hid_at(z - 1, y)
        else:
            target = side
        place = block_at(h, c)
        return pltpu.make_async_remote_copy(
            src_ref=place if src is None else src, dst_ref=place,
            send_sem=send_sem.at[link, h, c], recv_sem=recv_sem.at[h, c],
            device_id={"hid": target}, device_id_type=MESH,
        )

    def arrived(h, c):
        pltpu.make_async_remote_copy(
            src_ref=block_at(h, c), dst_ref=block_at(h, c),
            send_sem=send_sem.at[SIDE, h, c], recv_sem=recv_sem.at[h, c],
            device_id={"hid": side}, device_id_type=MESH,
        ).wait_recv()

    def pair(src, dst, k):
        return pltpu.make_async_remote_copy(
            src_ref=src, dst_ref=dst, send_sem=pair_sem.at[0, k], recv_sem=pair_sem.at[1, k],
            device_id={"wid": other}, device_id_type=MESH,
        )

    def own_sends(c, act):
        src = stats.at[me] if isinstance(c, int) and c == CHUNKS else tok_hbm.at[:, cols(c)]

        @pl.when(z + 1 < z_count)
        def _():
            act(send(me, c, UP, src))

        @pl.when(z > 0)
        def _():
            act(send(me, c, DOWN, src))

        act(send(me, c, SIDE, src))

    start = lambda copy: copy.start()
    ends = (z == 0).astype(jnp.int32) + (z == z_count - 1).astype(jnp.int32)
    pl.semaphore_wait(barrier, 4 - ends)
    for c in range(CHUNKS):
        own_sends(c, start)

    row_sum = jnp.zeros((own_rows, 1), jnp.float32)
    row_squares = jnp.zeros((own_rows, 1), jnp.float32)
    for c in range(CHUNKS):
        tok_copy(c).wait()
        block = gat[me, c].astype(jnp.float32)
        row_sum += jnp.sum(block, axis=1, keepdims=True)
        row_squares += jnp.sum(block * block, axis=1, keepdims=True)
    lane = lax.broadcasted_iota(jnp.int32, (own_rows, 128), 1)
    stat_mine[...] = jnp.where(lane < 64, row_sum, row_squares)

    stat_pair = pair(stat_mine, stat_other, 0)
    stat_pair.start()
    stat_pair.wait()
    both = stat_mine[...] + stat_other[...]
    row_mean = both[:, 0:1] / full_width
    variance = both[:, 64:65] / full_width - row_mean * row_mean
    stats[me] = jnp.where(lane < 64, row_mean, lax.rsqrt(variance + EPSILON))
    own_sends(CHUNKS, start)

    for copy in small[:3]:
        copy.wait()

    def normalised(h, c):
        stat = stats[h]
        block = gat[h, c].astype(jnp.float32)
        return ((block - stat[:, 0:1]) * stat[:, 64:65] * gain[:, cols(c)]).astype(jnp.bfloat16)

    kv_acc[...] = jnp.zeros_like(kv_acc)

    def kv_step(c, carry):
        kw_copy(c).wait()
        part = jnp.dot(normalised(me, c), kw[c], preferred_element_type=jnp.float32)
        kv_acc[...] += part.reshape(kv_acc.shape)
        return carry

    kv_pair = pair(kv_acc.at[other], kv_rx, 1)
    acc[...] = jnp.zeros_like(acc)

    def sources_at(k, visit):
        @pl.when(z - k >= 0)
        def _():
            visit(z - k, UP)

        @pl.when(z + k < z_count)
        def _():
            visit(z + k, DOWN)

    def for_sources(visit):
        for k in range(1, z_count):
            sources_at(k, visit)

    def onward(h, c, link, act):
        if link == UP:
            @pl.when(z + 1 < z_count)
            def _():
                act(send(h, c, UP))
        else:
            @pl.when(z > 0)
            def _():
                act(send(h, c, DOWN))

    def relay_at(k, c, act, wait):
        def visit(zz, link):
            h = hid_at(zz, y)
            if wait:
                arrived(h, c)
            onward(h, c, link, act)
            act(send(h, c, SIDE))

        sources_at(k, visit)

    def relay_last_side(c, act, wait):
        if wait:
            arrived(side, c)
        onward(side, c, UP, act)
        onward(side, c, DOWN, act)

    def relay_last_at(k, c, act, wait):
        def visit(zz, link):
            for yy in (y, 1 - y):
                h = hid_at(zz, yy)
                if wait:
                    arrived(h, c)
                onward(h, c, link, act)

        sources_at(k, visit)

    def arrived_side(c):
        arrived(side, c)

        def visit(zz, link):
            arrived(hid_at(zz, 1 - y), c)

        for_sources(visit)

    def normalise_all(c):
        def one(h, carry):
            normed[pl.ds(pl.multiple_of(h * own_rows, own_rows), own_rows), :] = normalised(h, c)
            return carry

        lax.fori_loop(0, hid_count, one, 0)

    def product(c, n):
        columns = pl.ds(pl.multiple_of(n * head_dim, head_dim), head_dim)
        part = jnp.dot(normed[...], qw[c, :, columns], preferred_element_type=jnp.float32)
        return part.reshape(acc.shape[1:])

    def compute(c):
        normalise_all(c)
        qw_copy(c).wait()

        def one(n, carry):
            acc[n] += product(c, n)
            return carry

        lax.fori_loop(0, tiles, one, 0)

    last = CHUNKS - 1
    final = last + z_count - 2
    for step in range(final + 1):
        done = step - (z_count - 1)
        if step == final:
            arrived_side(done)
            compute(done)
        for k in range(1, z_count):
            c = step - (k - 1)
            if 0 <= c < last:
                relay_at(k, c, start, True)
            elif c == last:
                relay_last_at(k, c, start, True)
        if step == min(2, last - 1):
            relay_last_side(last, start, True)
        if step < CHUNKS // 2:
            lax.fori_loop(2 * step, 2 * step + 2, kv_step, 0)
        if step == CHUNKS // 2 - 1:
            kv_pair.start()
        if 1 <= step < z_count:
            relay_at(step, CHUNKS, start, True)
        if step == z_count - 1:
            arrived_side(CHUNKS)
        if 0 <= done < last - 1:
            arrived_side(done)
            compute(done)
        if step == max(z_count - 1, CHUNKS // 2):
            kv_pair.wait()
            kv_new[...] = ((kv_acc[core] + kv_rx[...]) * ks[...]).astype(jnp.bfloat16)
            new_out = pltpu.make_async_copy(kv_new, new_ref, out_sem.at[0])
            new_out.start()

    def acc_copy(n):
        return pltpu.make_async_remote_copy(
            src_ref=acc.at[n, :, other], dst_ref=acc_rx.at[n],
            send_sem=acc_send.at[n], recv_sem=acc_recv.at[n],
            device_id={"wid": other}, device_id_type=MESH,
        )

    def q_copy(n, d):
        target = lax.rem(me + d, hid_count)
        return pltpu.make_async_remote_copy(
            src_ref=q_tx.at[n, target], dst_ref=q_rx.at[me * tiles + n],
            send_sem=q_send.at[n, d], recv_sem=q_recv.at[me * tiles + n],
            device_id={"hid": target}, device_id_type=MESH,
        )

    def q_arrived(h, n):
        pltpu.make_async_remote_copy(
            src_ref=q_tx.at[n, h], dst_ref=q_rx.at[h * tiles + n],
            send_sem=q_send.at[n, 0], recv_sem=q_recv.at[h * tiles + n],
            device_id={"hid": side}, device_id_type=MESH,
        ).wait_recv()

    normalise_all(last)
    qw_copy(last).wait()
    for n in range(tiles):
        acc[n] += product(last, n)
        acc_copy(n).start()
    for n in range(tiles):
        acc_copy(n).wait_recv()
        total = acc[n, :, core] + acc_rx[n]
        scale = qs[:, pl.ds(n * head_dim, head_dim)]
        q_tx[n] = (total * scale[None]).astype(jnp.bfloat16)
        for d in range(1, hid_count):
            q_copy(n, d).start()
        q_rx[me * tiles + n] = q_tx[n, me]

    finish = lambda copy: copy.wait_send()

    def drain(c, carry):
        own_sends(c, finish)
        return carry

    lax.fori_loop(0, CHUNKS, drain, 0)
    own_sends(CHUNKS, finish)

    def drain_relay(c, carry):
        for k in range(1, z_count):
            relay_at(k, c, finish, False)
        return carry

    lax.fori_loop(0, last, drain_relay, 0)
    relay_last_side(last, finish, False)
    for k in range(1, z_count):
        relay_at(k, CHUNKS, finish, False)
        relay_last_at(k, last, finish, False)
    for copy in small[3:]:
        copy.wait()

    for n in range(tiles):
        for d in range(1, hid_count):
            q_arrived(lax.rem(me + d, hid_count), n)

    heads = hid_count * tiles
    cache_len = keys.shape[1]
    inv_root = head_dim ** (-0.5)
    q_f32[...] = q_rx[...].astype(jnp.float32)
    position = lax.broadcasted_iota(jnp.int32, (heads, cache_len), 1)
    entries = kv_new[...].astype(jnp.float32)
    for r in range(req):
        query = q_f32[:, r, :]
        score = lax.dot_general(
            query.astype(jnp.bfloat16), keys[r], (((1,), (1,)), ((), ())),
            preferred_element_type=jnp.float32,
        ) * inv_root
        score = jnp.where(position < len_ref[r], score, -jnp.inf)
        own = jnp.sum(query * entries[r : r + 1, :head_dim], axis=1, keepdims=True) * inv_root
        peak = jnp.maximum(jnp.max(score, axis=1, keepdims=True), own)
        weight = jnp.exp(score - peak)
        own_weight = jnp.exp(own - peak)
        denom = jnp.sum(weight, axis=1, keepdims=True) + own_weight
        weight = (weight / denom).astype(jnp.bfloat16)
        own_weight = (own_weight / denom).astype(jnp.bfloat16).astype(jnp.float32)
        mixed = jnp.dot(weight, vals[r], preferred_element_type=jnp.float32)
        o_f32[:, r, :] = mixed + own_weight * entries[r : r + 1, head_dim:]
    for h in range(heads):
        att[:, h * head_dim : (h + 1) * head_dim] = o_f32[h].astype(jnp.bfloat16)
    att_out = pltpu.make_async_copy(att, att_ref, out_sem.at[1])
    att_out.start()
    for n in range(tiles):
        acc_copy(n).wait_send()
        for d in range(1, hid_count):
            q_copy(n, d).wait_send()
    new_out.wait()
    att_out.wait()


def hand_on(att_ref, new_ref, att_out, new_out):
    att_out[...] = att_ref[...]
    new_out[...] = new_ref[...]


def body(
    tokens, norm_gain, query_weight, query_scale, kv_weight, kv_scale,
    keys_cache, values_cache, lengths,
):
    hid_count = lax.axis_size("hid")
    wid_count = lax.axis_size("wid")
    own_rows, half_width = tokens.shape
    local_cols = query_weight.shape[1]
    req, cache_len, head_dim = keys_cache.shape
    tiles = local_cols // head_dim
    heads = hid_count * tiles
    width = half_width // CHUNKS
    kv_cols = kv_weight.shape[1]
    bf16, f32 = jnp.bfloat16, jnp.float32
    dma = pltpu.SemaphoreType.DMA
    vm = pltpu.VMEM
    scratch = [
        vm((hid_count, CHUNKS, own_rows, width), bf16),
        vm((1, half_width), f32),
        vm((CHUNKS, width, local_cols), bf16),
        vm((1, local_cols), f32),
        vm((CHUNKS, width, kv_cols), bf16),
        vm((1, kv_cols), f32),
        vm(keys_cache.shape, bf16),
        vm(values_cache.shape, bf16),
        vm((own_rows, 128), f32),
        vm((own_rows, 128), f32),
        vm((hid_count, own_rows, 128), f32),
        vm((hid_count * own_rows, width), bf16),
        vm((tiles, hid_count, wid_count, req, head_dim), f32),
        vm((tiles, hid_count, req, head_dim), f32),
        vm((wid_count, req, kv_cols), f32),
        vm((req, kv_cols), f32),
        vm((req, kv_cols), bf16),
        vm((tiles, hid_count, req, head_dim), bf16),
        vm((heads, req, head_dim), bf16),
        vm((heads, req, head_dim), f32),
        vm((heads, req, head_dim), f32),
        vm((req, heads * head_dim), bf16),
        dma((CHUNKS,)),
        dma((CHUNKS,)),
        dma((CHUNKS,)),
        dma((5,)),
        dma((3, hid_count, CHUNKS + 1)),
        dma((hid_count, CHUNKS + 1)),
        dma((2, 2)),
        dma((tiles,)),
        dma((tiles,)),
        dma((tiles, hid_count)),
        dma((heads,)),
        dma((2,)),
    ]
    hbm = pl.BlockSpec(memory_space=pl.ANY)
    attended, new_entries = pl.pallas_call(
        functools.partial(kernel, hid_count, wid_count),
        out_shape=(
            jax.ShapeDtypeStruct((req, heads * head_dim), bf16),
            jax.ShapeDtypeStruct((req, kv_cols), bf16),
        ),
        in_specs=[hbm] * 8 + [pl.BlockSpec(memory_space=pltpu.SMEM)],
        out_specs=(hbm, hbm),
        scratch_shapes=scratch,
        compiler_params=pltpu.CompilerParams(
            collective_id=0, has_side_effects=True, vmem_limit_bytes=60 * 1024 * 1024
        ),
    )(
        tokens, norm_gain.reshape(1, -1), query_weight, query_scale.reshape(1, -1),
        kv_weight, kv_scale.reshape(1, -1), keys_cache, values_cache, lengths,
    )
    whole = pl.BlockSpec(memory_space=pltpu.VMEM)
    return pl.pallas_call(
        hand_on,
        out_shape=(
            jax.ShapeDtypeStruct(attended.shape, bf16),
            jax.ShapeDtypeStruct(new_entries.shape, bf16),
        ),
        in_specs=[whole, whole],
        out_specs=(whole, whole),
    )(attended, new_entries)


def solution(mesh):
    placed = (
        P(("groups", "hid"), "wid"),
        P("wid"),
        P("wid", "hid"),
        P("hid"),
        P("wid", None),
        P(),
        P(("groups", "hid", "wid"), None, None),
        P(("groups", "hid", "wid"), None, None),
        P(("groups", "hid", "wid")),
    )
    return jax.shard_map(
        body,
        mesh=mesh,
        in_specs=placed,
        out_specs=(P(("groups", "hid", "wid"), None), P(("groups", "hid", "wid"), None)),
        check_vma=False,
    )
```

profile of v0, /device:TPU:0, one launch (start us, length us, event | category | flops | bytes accessed | tf_op | source)
XLA Modules:
  0.0 52.6 jit_solution(12856662076931933499)
XLA Ops:
  0.6 50.3 %shard_map.104 = (bf16[8,8192]{1,0:T(8,128)(2,1)}, bf16[8,512]{1,0:T(8,128)(2,1)}) custom-call(bf16[16,9216]{1,0:T(8,128)(2,1)} %tok_hbm.1, f32[1,9216]{1,0:T(1,128)} %bitcast.3, bf16[9216,1024]{1,0:T(8,128)(2,1)} %qw_hbm.1, f32[1,1024]{1,0:T(1,128)} %bitcast.4, bf16[9216,512]{1,0:T(8,128)(2,1)} %kw_hbm.1, f32[1,512]{1,0:T(1,128)} %bitcast.5, ...), custom_call_target="tpu_custom_call" | custom-call | tf_op jit(solution)/shard_map/pallas_call | solution.py:437
  51.0 1.6 %shard_map.105 = (bf16[8,8192]{1,0:T(8,128)(2,1)}, bf16[8,512]{1,0:T(8,128)(2,1)}) custom-call(bf16[8,8192]{1,0:T(8,128)(2,1)} %get-tuple-element.4.att_ref, bf16[8,512]{1,0:T(8,128)(2,1)} %get-tuple-element.5.new_ref), custom_call_target="tpu_custom_call" | custom-call | tf_op jit(solution)/shard_map/pallas_call | solution.py:454
where the time goes:
time: 52.7 us; the launch traced here: 52.6 us
  Pallas kernels  51.9 us (98%)
  between operations  0.64 us (1%)
    pallas_call x1, Pallas kernels, body(): pl.pallas_call(functools.partial(kernel, hid_count, wid_count), out_shape...  50.3 us
    pallas_call x1, Pallas kernels, body(): pl.pallas_call(hand_on, out_shape=(jax.ShapeDtypeStruct(attended.shape, b...  1.57 us

commit v1 on v0

v1 whole, which is shorter than its diff:
```python
import functools

import jax
import jax.numpy as jnp
from jax import lax
from jax.experimental import pallas as pl
from jax.experimental.pallas import tpu as pltpu
from jax.sharding import PartitionSpec as P

EPSILON = 1e-05
ROWS_Y = 2
TWELFTHS = (2, 2, 2, 2, 1, 1, 2)
AHEAD = 2
BEHIND = 2
TURN_OWN = 2
TURN_AT = 3
TURN_STEP = 2
UP, DOWN, SIDE = 0, 1, 2
MESH = pl.DeviceIdType.MESH


def kernel(
    hid_count, wid_count,
    tok_hbm, gain_hbm, qw_hbm, qs_hbm, kw_hbm, ks_hbm, keys_hbm, vals_hbm, len_hbm,
    att_ref, new_ref,
    tok, gain, qw, qs, kw, ks, keys, vals, lens,
    gat, stat_mine, stat_other, acc, acc_rx, kv_acc, kv_rx, kv_new,
    q_tx, q_rx, q_f32, o_f32, att,
    in_sem, pair_sem, send_sem, turn_send, line_sem, side_sem, turn_sem,
    acc_send, acc_recv, q_send, q_recv, out_sem,
):
    own_rows, half_width = tok_hbm.shape
    full_width = half_width * wid_count
    unit = half_width // sum(TWELFTHS)
    widths = [t * unit for t in TWELFTHS]
    starts = [sum(widths[:c]) for c in range(len(widths))]
    plain = len(widths) - 1
    turned = plain
    tiles, _, _, req, head_dim = acc.shape
    z_count = hid_count // ROWS_Y
    me = lax.axis_index("hid")
    core = lax.axis_index("wid")
    other = 1 - core
    z = me // ROWS_Y
    y = lax.rem(me, ROWS_Y)
    side = z * ROWS_Y + (1 - y)

    def hid_at(zz, yy):
        return zz * ROWS_Y + yy

    def cols(c):
        return pl.ds(starts[c], widths[c])

    tok_in = pltpu.make_async_copy(tok_hbm, tok, in_sem.at[0])
    gain_in = pltpu.make_async_copy(gain_hbm, gain, in_sem.at[1])
    kw_in = pltpu.make_async_copy(kw_hbm, kw, in_sem.at[2])
    qw_in = pltpu.make_async_copy(qw_hbm, qw, in_sem.at[3])
    late_in = [
        pltpu.make_async_copy(qs_hbm, qs, in_sem.at[4]),
        pltpu.make_async_copy(ks_hbm, ks, in_sem.at[5]),
        pltpu.make_async_copy(keys_hbm, keys, in_sem.at[6]),
        pltpu.make_async_copy(vals_hbm, vals, in_sem.at[7]),
        pltpu.make_async_copy(len_hbm, lens, in_sem.at[8]),
    ]
    tok_in.start()

    barrier = pltpu.get_barrier_semaphore()

    @pl.when(z + 1 < z_count)
    def _():
        pl.semaphore_signal(barrier, inc=1, device_id={"hid": hid_at(z + 1, y)}, device_id_type=MESH)

    @pl.when(z > 0)
    def _():
        pl.semaphore_signal(barrier, inc=1, device_id={"hid": hid_at(z - 1, y)}, device_id_type=MESH)

    pl.semaphore_signal(barrier, inc=1, device_id={"hid": side}, device_id_type=MESH)
    pl.semaphore_signal(barrier, inc=1, device_id={"wid": other}, device_id_type=MESH)
    gain_in.start()
    kw_in.start()
    qw_in.start()
    for copy in late_in:
        copy.start()

    tok_in.wait()
    row_sum = jnp.zeros((own_rows, 1), jnp.float32)
    row_squares = jnp.zeros((own_rows, 1), jnp.float32)
    for c in range(len(widths)):
        block = tok[:, cols(c)].astype(jnp.float32)
        row_sum += jnp.sum(block, axis=1, keepdims=True)
        row_squares += jnp.sum(block * block, axis=1, keepdims=True)
    lane = lax.broadcasted_iota(jnp.int32, (own_rows, 128), 1)
    stat_mine[...] = jnp.where(lane < 64, row_sum, row_squares)

    ends = (z == 0).astype(jnp.int32) + (z == z_count - 1).astype(jnp.int32)
    pl.semaphore_wait(barrier, 4 - ends)

    def pair(src, dst, k):
        return pltpu.make_async_remote_copy(
            src_ref=src, dst_ref=dst, send_sem=pair_sem.at[0, k], recv_sem=pair_sem.at[1, k],
            device_id={"wid": other}, device_id_type=MESH,
        )

    stat_pair = pair(stat_mine, stat_other, 0)
    stat_pair.start()
    gain_in.wait()
    stat_pair.wait()
    both = stat_mine[...] + stat_other[...]
    row_mean = both[:, 0:1] / full_width
    variance = both[:, 64:65] / full_width - row_mean * row_mean
    row_scale = lax.rsqrt(variance + EPSILON)

    def normalise(c):
        block = tok[:, cols(c)].astype(jnp.float32)
        gat[me, :, cols(c)] = (
            (block - row_mean) * row_scale * gain[:, cols(c)]
        ).astype(jnp.bfloat16)

    start = lambda copy: copy.start()
    finish = lambda copy: copy.wait_send()

    def target_of(link):
        if link == UP:
            return hid_at(z + 1, y)
        if link == DOWN:
            return hid_at(z - 1, y)
        return side

    def send(zz, c, link):
        place = gat.at[hid_at(zz, y), :, cols(c)]
        if link == SIDE:
            recv = side_sem.at[c]
        else:
            recv = line_sem.at[zz, c]
        return pltpu.make_async_remote_copy(
            src_ref=place, dst_ref=place, send_sem=send_sem.at[link, zz], recv_sem=recv,
            device_id={"hid": target_of(link)}, device_id_type=MESH,
        )

    def send_turned(zz, link):
        place = gat.at[hid_at(zz, 1 - y), :, cols(turned)]
        return pltpu.make_async_remote_copy(
            src_ref=place, dst_ref=place, send_sem=turn_send.at[link, zz], recv_sem=turn_sem.at[zz],
            device_id={"hid": target_of(link)}, device_id_type=MESH,
        )

    def arrived(place, sem):
        pltpu.make_async_remote_copy(
            src_ref=place, dst_ref=place, send_sem=send_sem.at[SIDE, 0], recv_sem=sem,
            device_id={"hid": side}, device_id_type=MESH,
        ).wait_recv()

    def line_arrived(zz, c):
        arrived(gat.at[hid_at(zz, y), :, cols(c)], line_sem.at[zz, c])

    def turned_arrived(zz):
        arrived(gat.at[hid_at(zz, 1 - y), :, cols(turned)], turn_sem.at[zz])

    def side_arrived(c):
        if c == turned:
            arrived(gat.at[side, :, cols(c)], side_sem.at[c])
        else:
            arrived(gat.at[pl.ds(0, z_count), :, cols(c)], side_sem.at[c])

    def onward(link, act):
        if link == UP:
            @pl.when(z + 1 < z_count)
            def _():
                act()
        else:
            @pl.when(z > 0)
            def _():
                act()

    def own_sends(c):
        for link in (UP, DOWN):
            onward(link, lambda: send(z, c, link).start())
        send(z, c, SIDE).start()

    def sources_at(k, visit):
        @pl.when(z - k >= 0)
        def _():
            visit(z - k, UP)

        @pl.when(z + k < z_count)
        def _():
            visit(z + k, DOWN)

    def relay(k, c):
        def visit(zz, link):
            line_arrived(zz, c)
            onward(link, lambda: send(zz, c, link).start())
            if c != turned:
                send(zz, c, SIDE).start()

        sources_at(k, visit)

    def relay_turned(k):
        def visit(zz, link):
            line_arrived(zz, turned)
            onward(link, lambda: send(zz, turned, link).start())
            turned_arrived(zz)
            onward(link, lambda: send_turned(zz, link).start())

        sources_at(k, visit)

    def turn():
        side_arrived(turned)
        for link in (UP, DOWN):
            onward(link, lambda: send_turned(z, link).start())

    own_order = list(range(TURN_OWN)) + [turned] + list(range(TURN_OWN, plain))
    pending = list(own_order)
    normalise(pending[0])
    for i in range(AHEAD):
        normalise(own_order[i + 1])
        own_sends(pending.pop(0))
    for c in own_order[AHEAD + 1 :]:
        normalise(c)

    kv_parts = len(widths)

    def kv_step(c):
        part = jnp.dot(gat[me, :, cols(c)], kw[cols(c), :], preferred_element_type=jnp.float32)
        part = part.reshape(kv_acc.shape)
        if c == 0:
            kv_acc[...] = part
        else:
            kv_acc[...] += part

    kv_pair = pair(kv_acc.at[other], kv_rx, 1)

    def operand(c):
        return gat[:, :, cols(c)].reshape(hid_count * own_rows, widths[c])

    def product(c, n):
        columns = pl.ds(pl.multiple_of(n * head_dim, head_dim), head_dim)
        part = jnp.dot(operand(c), qw[cols(c), columns], preferred_element_type=jnp.float32)
        return part.reshape(acc.shape[1:])

    def compute(c):
        def one(n, carry):
            if c == 0:
                acc[n] = product(c, n)
            else:
                acc[n] += product(c, n)
            return carry

        lax.fori_loop(0, tiles, one, 0)

    rounds = plain + z_count - 2 + max(BEHIND, 0)
    rounds = max(rounds, TURN_AT + 1 + TURN_STEP * (z_count - 1))
    kv_done = 0
    for r in range(rounds):
        if pending:
            own_sends(pending.pop(0))
        for k in range(1, z_count):
            c = r - (k - 1)
            if 0 <= c < plain:
                relay(k, c)
        if r == 0:
            kw_in.wait()
        for _ in range(2):
            if kv_done < kv_parts:
                kv_step(kv_done)
                kv_done += 1
                if kv_done == kv_parts:
                    kv_pair.start()
        if r == TURN_AT:
            turn()
        if r > TURN_AT and (r - TURN_AT) % TURN_STEP == 0:
            k = (r - TURN_AT) // TURN_STEP
            if 1 <= k < z_count:
                relay_turned(k)
        c = r - (z_count - 2) - BEHIND
        if c == 0:
            qw_in.wait()
        if 0 <= c < plain - 1:
            side_arrived(c)
            compute(c)
    kv_pair.wait()
    for copy in late_in:
        copy.wait()
    kv_new[...] = ((kv_acc[core] + kv_rx[...]) * ks[...]).astype(jnp.bfloat16)
    new_out = pltpu.make_async_copy(kv_new, new_ref, out_sem.at[0])
    new_out.start()
    for c in range(max(0, rounds - (z_count - 2) - BEHIND), plain - 1):
        side_arrived(c)
        compute(c)
    compute(turned)

    def acc_copy(n):
        return pltpu.make_async_remote_copy(
            src_ref=acc.at[n, :, other], dst_ref=acc_rx.at[n],
            send_sem=acc_send.at[0], recv_sem=acc_recv.at[n],
            device_id={"wid": other}, device_id_type=MESH,
        )

    def q_copy(n, d):
        target = lax.rem(me + d, hid_count)
        return pltpu.make_async_remote_copy(
            src_ref=q_tx.at[n, target], dst_ref=q_rx.at[n, me],
            send_sem=q_send.at[0], recv_sem=q_recv.at[n],
            device_id={"hid": target}, device_id_type=MESH,
        )

    last = plain - 1
    side_arrived(last)
    for n in range(tiles):
        acc[n] += product(last, n)
        acc_copy(n).start()
    for n in range(tiles):
        acc_copy(n).wait_recv()
        total = acc[n, :, core] + acc_rx[n]
        scale = qs[:, pl.ds(n * head_dim, head_dim)]
        q_tx[n] = (total * scale[None]).astype(jnp.bfloat16)
        for d in range(1, hid_count):
            q_copy(n, d).start()
        q_rx[n, me] = q_tx[n, me]

    def whole(zz, link):
        place = gat.at[hid_at(zz, y)]
        if link == SIDE:
            place = gat.at[hid_at(zz, y), :, pl.ds(0, starts[turned])]
        return pltpu.make_async_remote_copy(
            src_ref=place, dst_ref=place, send_sem=send_sem.at[link, zz], recv_sem=side_sem.at[0],
            device_id={"hid": side}, device_id_type=MESH,
        )

    own_place = gat.at[me]
    for link in (UP, DOWN):
        onward(link, lambda: whole(z, link).wait_send())
        onward(link, lambda: send_turned(z, link).wait_send())
    pltpu.make_async_remote_copy(
        src_ref=own_place, dst_ref=own_place, send_sem=send_sem.at[SIDE, z], recv_sem=side_sem.at[0],
        device_id={"hid": side}, device_id_type=MESH,
    ).wait_send()

    def drain(zz, link):
        onward(link, lambda: whole(zz, link).wait_send())
        onward(link, lambda: send_turned(zz, link).wait_send())
        whole(zz, SIDE).wait_send()

    for k in range(1, z_count):
        sources_at(k, drain)

    for n in range(tiles):
        place = q_rx.at[n, pl.ds(0, hid_count - 1)]
        pltpu.make_async_remote_copy(
            src_ref=place, dst_ref=place, send_sem=q_send.at[0], recv_sem=q_recv.at[n],
            device_id={"hid": side}, device_id_type=MESH,
        ).wait_recv()

    heads = hid_count * tiles
    cache_len = keys.shape[1]
    inv_root = head_dim ** (-0.5)
    for n in range(tiles):
        for h in range(hid_count):
            q_f32[h * tiles + n] = q_rx[n, h].astype(jnp.float32)
    position = lax.broadcasted_iota(jnp.int32, (heads, cache_len), 1)
    entries = kv_new[...].astype(jnp.float32)
    for r in range(req):
        query = q_f32[:, r, :]
        score = lax.dot_general(
            query.astype(jnp.bfloat16), keys[r], (((1,), (1,)), ((), ())),
            preferred_element_type=jnp.float32,
        ) * inv_root
        score = jnp.where(position < lens[r], score, -jnp.inf)
        own = jnp.sum(query * entries[r : r + 1, :head_dim], axis=1, keepdims=True) * inv_root
        peak = jnp.maximum(jnp.max(score, axis=1, keepdims=True), own)
        weight = jnp.exp(score - peak)
        own_weight = jnp.exp(own - peak)
        denom = jnp.sum(weight, axis=1, keepdims=True) + own_weight
        weight = (weight / denom).astype(jnp.bfloat16)
        own_weight = (own_weight / denom).astype(jnp.bfloat16).astype(jnp.float32)
        mixed = jnp.dot(weight, vals[r], preferred_element_type=jnp.float32)
        o_f32[:, r, :] = mixed + own_weight * entries[r : r + 1, head_dim:]
    for h in range(heads):
        att[:, h * head_dim : (h + 1) * head_dim] = o_f32[h].astype(jnp.bfloat16)
    att_out = pltpu.make_async_copy(att, att_ref, out_sem.at[1])
    att_out.start()
    sent = acc.at[:, :, other]
    pltpu.make_async_remote_copy(
        src_ref=sent, dst_ref=acc_rx, send_sem=acc_send.at[0], recv_sem=acc_recv.at[0],
        device_id={"wid": other}, device_id_type=MESH,
    ).wait_send()
    sent = q_tx.at[:, pl.ds(0, hid_count - 1)]
    pltpu.make_async_remote_copy(
        src_ref=sent, dst_ref=sent, send_sem=q_send.at[0], recv_sem=q_recv.at[0],
        device_id={"hid": side}, device_id_type=MESH,
    ).wait_send()
    new_out.wait()
    att_out.wait()


def hand_on(att_ref, new_ref, att_out, new_out):
    att_out[...] = att_ref[...]
    new_out[...] = new_ref[...]


def body(
    tokens, norm_gain, query_weight, query_scale, kv_weight, kv_scale,
    keys_cache, values_cache, lengths,
):
    hid_count = lax.axis_size("hid")
    wid_count = lax.axis_size("wid")
    own_rows, half_width = tokens.shape
    local_cols = query_weight.shape[1]
    req, cache_len, head_dim = keys_cache.shape
    tiles = local_cols // head_dim
    heads = hid_count * tiles
    z_count = hid_count // ROWS_Y
    chunks = len(TWELFTHS)
    kv_cols = kv_weight.shape[1]
    bf16, f32 = jnp.bfloat16, jnp.float32
    dma = pltpu.SemaphoreType.DMA
    vm = pltpu.VMEM
    scratch = [
        vm((own_rows, half_width), bf16),
        vm((1, half_width), f32),
        vm((half_width, local_cols), bf16),
        vm((1, local_cols), f32),
        vm((half_width, kv_cols), bf16),
        vm((1, kv_cols), f32),
        vm(keys_cache.shape, bf16),
        vm(values_cache.shape, bf16),
        pltpu.SMEM(lengths.shape, jnp.int32),
        vm((hid_count, own_rows, half_width), bf16),
        vm((own_rows, 128), f32),
        vm((own_rows, 128), f32),
        vm((tiles, hid_count, wid_count, req, head_dim), f32),
        vm((tiles, hid_count, req, head_dim), f32),
        vm((wid_count, req, kv_cols), f32),
        vm((req, kv_cols), f32),
        vm((req, kv_cols), bf16),
        vm((tiles, hid_count, req, head_dim), bf16),
        vm((tiles, hid_count, req, head_dim), bf16),
        vm((heads, req, head_dim), f32),
        vm((heads, req, head_dim), f32),
        vm((req, heads * head_dim), bf16),
        dma((9,)),
        dma((2, 2)),
        dma((3, z_count)),
        dma((2, z_count)),
        dma((z_count, chunks)),
        dma((chunks,)),
        dma((z_count,)),
        dma((1,)),
        dma((tiles,)),
        dma((1,)),
        dma((tiles,)),
        dma((2,)),
    ]
    hbm = pl.BlockSpec(memory_space=pl.ANY)
    attended, new_entries = pl.pallas_call(
        functools.partial(kernel, hid_count, wid_count),
        out_shape=(
            jax.ShapeDtypeStruct((req, heads * head_dim), bf16),
            jax.ShapeDtypeStruct((req, kv_cols), bf16),
        ),
        in_specs=[hbm] * 9,
        out_specs=(hbm, hbm),
        scratch_shapes=scratch,
        compiler_params=pltpu.CompilerParams(
            collective_id=0, has_side_effects=True, vmem_limit_bytes=60 * 1024 * 1024
        ),
    )(
        tokens, norm_gain.reshape(1, -1), query_weight, query_scale.reshape(1, -1),
        kv_weight, kv_scale.reshape(1, -1), keys_cache, values_cache, lengths,
    )
    whole = pl.BlockSpec(memory_space=pltpu.VMEM)
    return pl.pallas_call(
        hand_on,
        out_shape=(
            jax.ShapeDtypeStruct(attended.shape, bf16),
            jax.ShapeDtypeStruct(new_entries.shape, bf16),
        ),
        in_specs=[whole, whole],
        out_specs=(whole, whole),
    )(attended, new_entries)


def solution(mesh):
    placed = (
        P(("groups", "hid"), "wid"),
        P("wid"),
        P("wid", "hid"),
        P("hid"),
        P("wid", None),
        P(),
        P(("groups", "hid", "wid"), None, None),
        P(("groups", "hid", "wid"), None, None),
        P(("groups", "hid", "wid")),
    )
    return jax.shard_map(
        body,
        mesh=mesh,
        in_specs=placed,
        out_specs=(P(("groups", "hid", "wid"), None), P(("groups", "hid", "wid"), None)),
        check_vma=False,
    )
```

time: 52.7 us -> 46.2 us (0.88)
  Pallas kernels: 51.9 us -> 45.4 us
    pallas_call x1, Pallas kernels: 50.3 us -> 43.9 us  [body(): pl.pallas_call(functools.partial(kernel, hid_count, wid_count), out_shape...]
where the time goes in v1:
time: 46.2 us; the launch traced here: 46.1 us
  Pallas kernels  45.4 us (98%)
  between operations  0.64 us (1%)
    pallas_call x1, Pallas kernels, body(): pl.pallas_call(functools.partial(kernel, hid_count, wid_count), out_shape...  43.9 us
    pallas_call x1, Pallas kernels, body(): pl.pallas_call(hand_on, out_shape=(jax.ShapeDtypeStruct(attended.shape, b...  1.57 us

profile of v1, /device:TPU:0, one launch (start us, length us, event | category | flops | bytes accessed | tf_op | source)
XLA Modules:
  0.0 46.1 jit_solution(16936502212420984338)
XLA Ops:
  0.6 43.9 %shard_map.104 = (bf16[8,8192]{1,0:T(8,128)(2,1)}, bf16[8,512]{1,0:T(8,128)(2,1)}) custom-call(bf16[16,9216]{1,0:T(8,128)(2,1)} %tok_hbm.1, f32[1,9216]{1,0:T(1,128)} %bitcast.3, bf16[9216,1024]{1,0:T(8,128)(2,1)} %qw_hbm.1, f32[1,1024]{1,0:T(1,128)} %bitcast.4, bf16[9216,512]{1,0:T(8,128)(2,1)} %kw_hbm.1, f32[1,512]{1,0:T(1,128)} %bitcast.5, ...), custom_call_target="tpu_custom_call" | custom-call | tf_op jit(solution)/shard_map/pallas_call | solution.py:455
  44.5 1.6 %shard_map.105 = (bf16[8,8192]{1,0:T(8,128)(2,1)}, bf16[8,512]{1,0:T(8,128)(2,1)}) custom-call(bf16[8,8192]{1,0:T(8,128)(2,1)} %get-tuple-element.4.att_ref, bf16[8,512]{1,0:T(8,128)(2,1)} %get-tuple-element.5.new_ref), custom_call_target="tpu_custom_call" | custom-call | tf_op jit(solution)/shard_map/pallas_call | solution.py:472

commit v2 on v1

--- a/solution.py
+++ b/solution.py
@@ -25,7 +25,7 @@
     att_ref, new_ref,
     tok, gain, qw, qs, kw, ks, keys, vals, lens,
     gat, stat_mine, stat_other, acc, acc_rx, kv_acc, kv_rx, kv_new,
-    q_tx, q_rx, q_f32, o_f32, att,
+    q_tx, q_rx, q_f32, o_f32, scores, weights, att,
     in_sem, pair_sem, send_sem, turn_send, line_sem, side_sem, turn_sem,
     acc_send, acc_recv, q_send, q_recv, out_sem,
 ):
@@ -359,22 +359,39 @@
             q_f32[h * tiles + n] = q_rx[n, h].astype(jnp.float32)
     position = lax.broadcasted_iota(jnp.int32, (heads, cache_len), 1)
     entries = kv_new[...].astype(jnp.float32)
+    def query_of(r):
+        return q_f32[:, r, :]
+
+    def score(r):
+        scores[r] = lax.dot_general(
+            query_of(r).astype(jnp.bfloat16), keys[r], (((1,), (1,)), ((), ())),
+            preferred_element_type=jnp.float32,
+        )
+
+    def weigh(r):
+        live = jnp.where(position < lens[r], scores[r] * inv_root, -jnp.inf)
+        own = jnp.sum(query_of(r) * entries[r : r + 1, :head_dim], axis=1, keepdims=True) * inv_root
+        peak = jnp.maximum(jnp.max(live, axis=1, keepdims=True), own)
+        weight = jnp.exp(live - peak)
+        own_weight = jnp.exp(own - peak)
+        inverse = 1.0 / (jnp.sum(weight, axis=1, keepdims=True) + own_weight)
+        weights[r] = (weight * inverse).astype(jnp.bfloat16)
+        return (own_weight * inverse).astype(jnp.bfloat16).astype(jnp.float32)
+
+    def mix(r, own_weight):
+        mixed = jnp.dot(weights[r], vals[r], preferred_element_type=jnp.float32)
+        o_f32[:, r, :] = mixed + own_weight * entries[r : r + 1, head_dim:]
+
+    own_weights = []
+    for r in range(min(2, req)):
+        score(r)
     for r in range(req):
-        query = q_f32[:, r, :]
-        score = lax.dot_general(
-            query.astype(jnp.bfloat16), keys[r], (((1,), (1,)), ((), ())),
-            preferred_element_type=jnp.float32,
-        ) * inv_root
-        score = jnp.where(position < lens[r], score, -jnp.inf)
-        own = jnp.sum(query * entries[r : r + 1, :head_dim], axis=1, keepdims=True) * inv_root
-        peak = jnp.maximum(jnp.max(score, axis=1, keepdims=True), own)
-        weight = jnp.exp(score - peak)
-        own_weight = jnp.exp(own - peak)
-        denom = jnp.sum(weight, axis=1, keepdims=True) + own_weight
-        weight = (weight / denom).astype(jnp.bfloat16)
-        own_weight = (own_weight / denom).astype(jnp.bfloat16).astype(jnp.float32)
-        mixed = jnp.dot(weight, vals[r], preferred_element_type=jnp.float32)
-        o_f32[:, r, :] = mixed + own_weight * entries[r : r + 1, head_dim:]
+        own_weights.append(weigh(r))
+        if r + 2 < req:
+            score(r + 2)
+        if r >= 1:
+            mix(r - 1, own_weights[r - 1])
+    mix(req - 1, own_weights[req - 1])
     for h in range(heads):
         att[:, h * head_dim : (h + 1) * head_dim] = o_f32[h].astype(jnp.bfloat16)
     att_out = pltpu.make_async_copy(att, att_ref, out_sem.at[1])
@@ -437,6 +454,8 @@
         vm((tiles, hid_count, req, head_dim), bf16),
         vm((heads, req, head_dim), f32),
         vm((heads, req, head_dim), f32),
+        vm((req, heads, cache_len), f32),
+        vm((req, heads, cache_len), bf16),
         vm((req, heads * head_dim), bf16),
         dma((9,)),
         dma((2, 2)),

time: 46.2 us -> 44.2 us (0.957)
  Pallas kernels: 45.4 us -> 43.4 us
    pallas_call x1, Pallas kernels: 43.9 us -> 41.8 us  [body(): pl.pallas_call(functools.partial(kernel, hid_count, wid_count), out_shape...]
where the time goes in v2:
time: 44.2 us; the launch traced here: 44 us
  Pallas kernels  43.4 us (98%)
  between operations  0.64 us (1%)
    pallas_call x1, Pallas kernels, body(): pl.pallas_call(functools.partial(kernel, hid_count, wid_count), out_shape...  41.8 us
    pallas_call x1, Pallas kernels, body(): pl.pallas_call(hand_on, out_shape=(jax.ShapeDtypeStruct(attended.shape, b...  1.57 us

profile of v2, /device:TPU:0, one launch (start us, length us, event | category | flops | bytes accessed | tf_op | source)
XLA Modules:
  0.0 44.0 jit_solution(8441579585702839833)
XLA Ops:
  0.6 41.8 %shard_map.104 = (bf16[8,8192]{1,0:T(8,128)(2,1)}, bf16[8,512]{1,0:T(8,128)(2,1)}) custom-call(bf16[16,9216]{1,0:T(8,128)(2,1)} %tok_hbm.1, f32[1,9216]{1,0:T(1,128)} %bitcast.3, bf16[9216,1024]{1,0:T(8,128)(2,1)} %qw_hbm.1, f32[1,1024]{1,0:T(1,128)} %bitcast.4, bf16[9216,512]{1,0:T(8,128)(2,1)} %kw_hbm.1, f32[1,512]{1,0:T(1,128)} %bitcast.5, ...), custom_call_target="tpu_custom_call" | custom-call | tf_op jit(solution)/shard_map/pallas_call | solution.py:474
  42.5 1.6 %shard_map.105 = (bf16[8,8192]{1,0:T(8,128)(2,1)}, bf16[8,512]{1,0:T(8,128)(2,1)}) custom-call(bf16[8,8192]{1,0:T(8,128)(2,1)} %get-tuple-element.4.att_ref, bf16[8,512]{1,0:T(8,128)(2,1)} %get-tuple-element.5.new_ref), custom_call_target="tpu_custom_call" | custom-call | tf_op jit(solution)/shard_map/pallas_call | solution.py:491

commit v3 on v2

--- a/solution.py
+++ b/solution.py
@@ -9,7 +9,9 @@
 
 EPSILON = 1e-05
 ROWS_Y = 2
-TWELFTHS = (2, 2, 2, 2, 1, 1, 2)
+TWELFTHS = (3, 1, 2, 2, 1, 1, 2)
+LANES = 128
+BLOCK = 4
 AHEAD = 2
 BEHIND = 2
 TURN_OWN = 2
@@ -25,7 +27,7 @@
     att_ref, new_ref,
     tok, gain, qw, qs, kw, ks, keys, vals, lens,
     gat, stat_mine, stat_other, acc, acc_rx, kv_acc, kv_rx, kv_new,
-    q_tx, q_rx, q_f32, o_f32, scores, weights, att,
+    q_tx, q_rx, q_f32, o_f32, scores, weights, att, first,
     in_sem, pair_sem, send_sem, turn_send, line_sem, side_sem, turn_sem,
     acc_send, acc_recv, q_send, q_recv, out_sem,
 ):
@@ -51,6 +53,14 @@
     def cols(c):
         return pl.ds(starts[c], widths[c])
 
+    def held(c):
+        return pl.ds(starts[c] + (LANES if c > 1 else 0), widths[c])
+
+    def sent(c):
+        return pl.ds(held(c).start, widths[c] + (LANES if c == 1 else 0))
+
+    beside = pl.ds(starts[2], LANES)
+
     tok_in = pltpu.make_async_copy(tok_hbm, tok, in_sem.at[0])
     gain_in = pltpu.make_async_copy(gain_hbm, gain, in_sem.at[1])
     kw_in = pltpu.make_async_copy(kw_hbm, kw, in_sem.at[2])
@@ -101,24 +111,6 @@
             device_id={"wid": other}, device_id_type=MESH,
         )
 
-    stat_pair = pair(stat_mine, stat_other, 0)
-    stat_pair.start()
-    gain_in.wait()
-    stat_pair.wait()
-    both = stat_mine[...] + stat_other[...]
-    row_mean = both[:, 0:1] / full_width
-    variance = both[:, 64:65] / full_width - row_mean * row_mean
-    row_scale = lax.rsqrt(variance + EPSILON)
-
-    def normalise(c):
-        block = tok[:, cols(c)].astype(jnp.float32)
-        gat[me, :, cols(c)] = (
-            (block - row_mean) * row_scale * gain[:, cols(c)]
-        ).astype(jnp.bfloat16)
-
-    start = lambda copy: copy.start()
-    finish = lambda copy: copy.wait_send()
-
     def target_of(link):
         if link == UP:
             return hid_at(z + 1, y)
@@ -126,19 +118,20 @@
             return hid_at(z - 1, y)
         return side
 
-    def send(zz, c, link):
-        place = gat.at[hid_at(zz, y), :, cols(c)]
+    def send(zz, c, link, own=False):
+        place = gat.at[hid_at(zz, y), :, sent(c)]
+        source = tok.at[:, cols(0)] if own and c == 0 else place
         if link == SIDE:
             recv = side_sem.at[c]
         else:
             recv = line_sem.at[zz, c]
         return pltpu.make_async_remote_copy(
-            src_ref=place, dst_ref=place, send_sem=send_sem.at[link, zz], recv_sem=recv,
+            src_ref=source, dst_ref=place, send_sem=send_sem.at[link, zz], recv_sem=recv,
             device_id={"hid": target_of(link)}, device_id_type=MESH,
         )
 
     def send_turned(zz, link):
-        place = gat.at[hid_at(zz, 1 - y), :, cols(turned)]
+        place = gat.at[hid_at(zz, 1 - y), :, sent(turned)]
         return pltpu.make_async_remote_copy(
             src_ref=place, dst_ref=place, send_sem=turn_send.at[link, zz], recv_sem=turn_sem.at[zz],
             device_id={"hid": target_of(link)}, device_id_type=MESH,
@@ -151,16 +144,16 @@
         ).wait_recv()
 
     def line_arrived(zz, c):
-        arrived(gat.at[hid_at(zz, y), :, cols(c)], line_sem.at[zz, c])
+        arrived(gat.at[hid_at(zz, y), :, sent(c)], line_sem.at[zz, c])
 
     def turned_arrived(zz):
-        arrived(gat.at[hid_at(zz, 1 - y), :, cols(turned)], turn_sem.at[zz])
+        arrived(gat.at[hid_at(zz, 1 - y), :, sent(turned)], turn_sem.at[zz])
 
     def side_arrived(c):
         if c == turned:
-            arrived(gat.at[side, :, cols(c)], side_sem.at[c])
+            arrived(gat.at[side, :, sent(c)], side_sem.at[c])
         else:
-            arrived(gat.at[pl.ds(0, z_count), :, cols(c)], side_sem.at[c])
+            arrived(gat.at[pl.ds(0, z_count), :, sent(c)], side_sem.at[c])
 
     def onward(link, act):
         if link == UP:
@@ -174,8 +167,8 @@
 
     def own_sends(c):
         for link in (UP, DOWN):
-            onward(link, lambda: send(z, c, link).start())
-        send(z, c, SIDE).start()
+            onward(link, lambda: send(z, c, link, True).start())
+        send(z, c, SIDE, True).start()
 
     def sources_at(k, visit):
         @pl.when(z - k >= 0)
@@ -211,17 +204,62 @@
 
     own_order = list(range(TURN_OWN)) + [turned] + list(range(TURN_OWN, plain))
     pending = list(own_order)
-    normalise(pending[0])
-    for i in range(AHEAD):
+    own_sends(pending.pop(0))
+    stat_pair = pair(stat_mine, stat_other, 0)
+    stat_pair.start()
+    gain_in.wait()
+    stat_pair.wait()
+    both = stat_mine[...] + stat_other[...]
+    row_mean = both[:, 0:1] / full_width
+    variance = both[:, 64:65] / full_width - row_mean * row_mean
+    row_scale = lax.rsqrt(variance + EPSILON)
+
+    def normalise(c):
+        block = tok[:, cols(c)].astype(jnp.float32)
+        value = ((block - row_mean) * row_scale * gain[:, cols(c)]).astype(jnp.bfloat16)
+        if c == 0:
+            first[me] = value
+        else:
+            gat[me, :, held(c)] = value
+
+    def addends(value):
+        high = value.astype(jnp.bfloat16).astype(jnp.float32)
+        middle = (value - high).astype(jnp.bfloat16).astype(jnp.float32)
+        return high, middle, value - high - middle
+
+    def tell():
+        told = jnp.zeros((own_rows, LANES), jnp.float32)
+        for i, value in enumerate(addends(row_mean) + addends(row_scale)):
+            told = jnp.where(lane == i, value, told)
+        gat[me, :, beside] = told.astype(jnp.bfloat16)
+
+    def normalise_first():
+        def one(h, carry):
+            @pl.when(h != me)
+            def _():
+                told = gat[h, :, beside].astype(jnp.float32)
+                mean = told[:, 0:1] + told[:, 1:2] + told[:, 2:3]
+                scale = told[:, 3:4] + told[:, 4:5] + told[:, 5:6]
+                block = gat[h, :, held(0)].astype(jnp.float32)
+                first[h] = ((block - mean) * scale * gain[:, cols(0)]).astype(jnp.bfloat16)
+
+            return carry
+
+        lax.fori_loop(0, hid_count, one, 0)
+
+    normalise(1)
+    tell()
+    for i in range(1, AHEAD):
         normalise(own_order[i + 1])
         own_sends(pending.pop(0))
-    for c in own_order[AHEAD + 1 :]:
+    for c in own_order[AHEAD + 1 :] + [0]:
         normalise(c)
 
     kv_parts = len(widths)
 
     def kv_step(c):
-        part = jnp.dot(gat[me, :, cols(c)], kw[cols(c), :], preferred_element_type=jnp.float32)
+        rows = first[me] if c == 0 else gat[me, :, held(c)]
+        part = jnp.dot(rows, kw[cols(c), :], preferred_element_type=jnp.float32)
         part = part.reshape(kv_acc.shape)
         if c == 0:
             kv_acc[...] = part
@@ -231,22 +269,19 @@
     kv_pair = pair(kv_acc.at[other], kv_rx, 1)
 
     def operand(c):
-        return gat[:, :, cols(c)].reshape(hid_count * own_rows, widths[c])
-
-    def product(c, n):
-        columns = pl.ds(pl.multiple_of(n * head_dim, head_dim), head_dim)
+        rows = first[...] if c == 0 else gat[:, :, held(c)]
+        return rows.reshape(hid_count * own_rows, widths[c])
+
+    def add_product(c, low, high, fresh=False):
+        columns = pl.ds(low * head_dim, (high - low) * head_dim)
         part = jnp.dot(operand(c), qw[cols(c), columns], preferred_element_type=jnp.float32)
-        return part.reshape(acc.shape[1:])
-
-    def compute(c):
-        def one(n, carry):
-            if c == 0:
-                acc[n] = product(c, n)
-            else:
-                acc[n] += product(c, n)
-            return carry
-
-        lax.fori_loop(0, tiles, one, 0)
+        for n in range(low, high):
+            own = part[:, (n - low) * head_dim : (n - low + 1) * head_dim].reshape(acc.shape[1:])
+            acc[n] = own if fresh else acc[n] + own
+
+    def compute(c, fresh=False):
+        for low in range(0, tiles, BLOCK):
+            add_product(c, low, min(low + BLOCK, tiles), fresh)
 
     rounds = plain + z_count - 2 + max(BEHIND, 0)
     rounds = max(rounds, TURN_AT + 1 + TURN_STEP * (z_count - 1))
@@ -273,9 +308,14 @@
             if 1 <= k < z_count:
                 relay_turned(k)
         c = r - (z_count - 2) - BEHIND
-        if c == 0:
+        if c == 1:
             qw_in.wait()
-        if 0 <= c < plain - 1:
+            side_arrived(0)
+            side_arrived(1)
+            normalise_first()
+            compute(1, True)
+            compute(0)
+        elif 1 < c < plain - 1:
             side_arrived(c)
             compute(c)
     kv_pair.wait()
@@ -296,8 +336,7 @@
             device_id={"wid": other}, device_id_type=MESH,
         )
 
-    def q_copy(n, d):
-        target = lax.rem(me + d, hid_count)
+    def q_copy(n, target):
         return pltpu.make_async_remote_copy(
             src_ref=q_tx.at[n, target], dst_ref=q_rx.at[n, me],
             send_sem=q_send.at[0], recv_sem=q_recv.at[n],
@@ -306,22 +345,30 @@
 
     last = plain - 1
     side_arrived(last)
-    for n in range(tiles):
-        acc[n] += product(last, n)
-        acc_copy(n).start()
+    half = -(-tiles // 2)
+    for low in range(0, tiles, half):
+        high = min(low + half, tiles)
+        add_product(last, low, high)
+        for n in range(low, high):
+            acc_copy(n).start()
     for n in range(tiles):
         acc_copy(n).wait_recv()
         total = acc[n, :, core] + acc_rx[n]
         scale = qs[:, pl.ds(n * head_dim, head_dim)]
         q_tx[n] = (total * scale[None]).astype(jnp.bfloat16)
-        for d in range(1, hid_count):
-            q_copy(n, d).start()
+        for k in range(z_count - 1, 0, -1):
+            def hand_out(zz, link, n=n):
+                for yy in (1 - y, y):
+                    q_copy(n, hid_at(zz, yy)).start()
+
+            sources_at(k, hand_out)
+        q_copy(n, side).start()
         q_rx[n, me] = q_tx[n, me]
 
     def whole(zz, link):
         place = gat.at[hid_at(zz, y)]
         if link == SIDE:
-            place = gat.at[hid_at(zz, y), :, pl.ds(0, starts[turned])]
+            place = gat.at[hid_at(zz, y), :, pl.ds(0, sent(turned).start)]
         return pltpu.make_async_remote_copy(
             src_ref=place, dst_ref=place, send_sem=send_sem.at[link, zz], recv_sem=side_sem.at[0],
             device_id={"hid": side}, device_id_type=MESH,
@@ -396,14 +443,14 @@
         att[:, h * head_dim : (h + 1) * head_dim] = o_f32[h].astype(jnp.bfloat16)
     att_out = pltpu.make_async_copy(att, att_ref, out_sem.at[1])
     att_out.start()
-    sent = acc.at[:, :, other]
+    place = acc.at[:, :, other]
     pltpu.make_async_remote_copy(
-        src_ref=sent, dst_ref=acc_rx, send_sem=acc_send.at[0], recv_sem=acc_recv.at[0],
+        src_ref=place, dst_ref=acc_rx, send_sem=acc_send.at[0], recv_sem=acc_recv.at[0],
         device_id={"wid": other}, device_id_type=MESH,
     ).wait_send()
-    sent = q_tx.at[:, pl.ds(0, hid_count - 1)]
+    place = q_tx.at[:, pl.ds(0, hid_count - 1)]
     pltpu.make_async_remote_copy(
-        src_ref=sent, dst_ref=sent, send_sem=q_send.at[0], recv_sem=q_recv.at[0],
+        src_ref=place, dst_ref=place, send_sem=q_send.at[0], recv_sem=q_recv.at[0],
         device_id={"hid": side}, device_id_type=MESH,
     ).wait_send()
     new_out.wait()
@@ -442,7 +489,7 @@
         vm(keys_cache.shape, bf16),
         vm(values_cache.shape, bf16),
         pltpu.SMEM(lengths.shape, jnp.int32),
-        vm((hid_count, own_rows, half_width), bf16),
+        vm((hid_count, own_rows, half_width + LANES), bf16),
         vm((own_rows, 128), f32),
         vm((own_rows, 128), f32),
         vm((tiles, hid_count, wid_count, req, head_dim), f32),
@@ -457,6 +504,7 @@
         vm((req, heads, cache_len), f32),
         vm((req, heads, cache_len), bf16),
         vm((req, heads * head_dim), bf16),
+        vm((hid_count, own_rows, TWELFTHS[0] * half_width // sum(TWELFTHS)), bf16),
         dma((9,)),
         dma((2, 2)),
         dma((3, z_count)),

time: 44.2 us -> 41.3 us (0.934)
  Pallas kernels: 43.4 us -> 40.5 us
    pallas_call x1, Pallas kernels: 41.8 us -> 38.9 us  [body(): pl.pallas_call(functools.partial(kernel, hid_count, wid_count), out_shape...]
where the time goes in v3:
time: 41.3 us; the launch traced here: 41.1 us
  Pallas kernels  40.5 us (98%)
  between operations  0.64 us (2%)
    pallas_call x1, Pallas kernels, body(): pl.pallas_call(functools.partial(kernel, hid_count, wid_count), out_shape...  38.9 us
    pallas_call x1, Pallas kernels, body(): pl.pallas_call(hand_on, out_shape=(jax.ShapeDtypeStruct(attended.shape, b...  1.57 us

profile of v3, /device:TPU:0, one launch (start us, length us, event | category | flops | bytes accessed | tf_op | source)
XLA Modules:
  0.0 41.1 jit_solution(14274346935834958850)
XLA Ops:
  0.6 38.9 %shard_map.104 = (bf16[8,8192]{1,0:T(8,128)(2,1)}, bf16[8,512]{1,0:T(8,128)(2,1)}) custom-call(bf16[16,9216]{1,0:T(8,128)(2,1)} %tok_hbm.1, f32[1,9216]{1,0:T(1,128)} %bitcast.3, bf16[9216,1024]{1,0:T(8,128)(2,1)} %qw_hbm.1, f32[1,1024]{1,0:T(1,128)} %bitcast.4, bf16[9216,512]{1,0:T(8,128)(2,1)} %kw_hbm.1, f32[1,512]{1,0:T(1,128)} %bitcast.5, ...), custom_call_target="tpu_custom_call" | custom-call | tf_op jit(solution)/shard_map/pallas_call | solution.py:522
  39.6 1.6 %shard_map.105 = (bf16[8,8192]{1,0:T(8,128)(2,1)}, bf16[8,512]{1,0:T(8,128)(2,1)}) custom-call(bf16[8,8192]{1,0:T(8,128)(2,1)} %get-tuple-element.4.att_ref, bf16[8,512]{1,0:T(8,128)(2,1)} %get-tuple-element.5.new_ref), custom_call_target="tpu_custom_call" | custom-call | tf_op jit(solution)/shard_map/pallas_call | solution.py:539
